TPU v7x, 32 devices: a whole 2x2x4 slice. The times are simulated.
32 devices in a mesh: seq: 4 (over y, x), fsdp: 8 (over z, core).
Axes of the slice: x: 2, y: 2, z: 4, core: 2. Of those that a mesh axis runs over, the one named last changes fastest.
Arguments:
- tokens: bfloat16 [8, 1024, 1024], P('fsdp', 'seq'), may hold values from -6 to 6
- segments: int32 [8, 1024], P('fsdp', 'seq'), may hold values from 0 to 2, as said below
- qkv_weight: bfloat16 [1024, 3072], P(('seq', 'fsdp')), may hold values from -0.1875 to 0.1875
- out_weight: bfloat16 [1024, 1024], P(('seq', 'fsdp')), may hold values from -0.1875 to 0.1875
- up_weight: bfloat16 [1024, 4096], P(('seq', 'fsdp')), may hold values from -0.1875 to 0.1875
- up_bias: bfloat16 [4096], P(('seq', 'fsdp')), may hold values from -3 to 3
- down_weight: bfloat16 [4096, 1024], P(('seq', 'fsdp')), may hold values from -0.09375 to 0.09375
- first_gain: bfloat16 [1024], P(('seq', 'fsdp')), may hold values from 0.5 to 1.5
- first_shift: bfloat16 [1024], P(('seq', 'fsdp')), may hold values from -3 to 3
- second_gain: bfloat16 [1024], P(('seq', 'fsdp')), may hold values from 0.5 to 1.5
- second_shift: bfloat16 [1024], P(('seq', 'fsdp')), may hold values from -3 to 3
- third_gain: bfloat16 [1024], P(('seq', 'fsdp')), may hold values from 0.5 to 1.5
- third_shift: bfloat16 [1024], P(('seq', 'fsdp')), may hold values from -3 to 3
- fourth_gain: bfloat16 [1024], P(('seq', 'fsdp')), may hold values from 0.5 to 1.5
- fourth_shift: bfloat16 [1024], P(('seq', 'fsdp')), may hold values from -3 to 3
- out_cotangent: bfloat16 [8, 1024, 1024], P('fsdp', 'seq'), may hold values from -6 to 6
Outputs:
- layer_out: bfloat16 [8, 1024, 1024], P('fsdp', 'seq')
- tokens_grad: float32 [8, 1024, 1024], P('fsdp', 'seq')
- qkv_weight_grad: float32 [1024, 3072], P(('seq', 'fsdp'))
- out_weight_grad: float32 [1024, 1024], P(('seq', 'fsdp'))
- up_weight_grad: float32 [1024, 4096], P(('seq', 'fsdp'))
- up_bias_grad: float32 [4096], P(('seq', 'fsdp'))
- down_weight_grad: float32 [4096, 1024], P(('seq', 'fsdp'))
- first_gain_grad: float32 [1024], P(('seq', 'fsdp'))
- first_shift_grad: float32 [1024], P(('seq', 'fsdp'))
- second_gain_grad: float32 [1024], P(('seq', 'fsdp'))
- second_shift_grad: float32 [1024], P(('seq', 'fsdp'))
- third_gain_grad: float32 [1024], P(('seq', 'fsdp'))
- third_shift_grad: float32 [1024], P(('seq', 'fsdp'))
- fourth_gain_grad: float32 [1024], P(('seq', 'fsdp'))
- fourth_shift_grad: float32 [1024], P(('seq', 'fsdp'))
Inputs may be any that keep to these rules, and one draw needn't show every extreme that they name: `segments`: within a sequence document numbers never fall; each sequence holds 3 documents of 200 to 512 tokens, one of exactly 512.
All inputs are finite; a program needn't handle non-finite values.
Results may differ from a plain program's by a relative error of at most 0.012.
Values may be sent and summed in bfloat16 or wider, within the bound.
A program may use at most 192 MiB of HBM per device.

v0:
```python
from functools import partial
import jax
import jax.numpy as jnp
from jax import lax
from jax.sharding import PartitionSpec as P

HEAD_DIM = 64
F32 = jnp.float32
BF16 = jnp.bfloat16


def layer_norm(value, gain, shift):
    center = value - jnp.mean(value, -1, keepdims=True)
    spread = jnp.mean(center * center, -1, keepdims=True)
    return center * lax.rsqrt(spread + 1e-05) * gain + shift


def norm_pull(value, gain, grad):
    center = value - jnp.mean(value, -1, keepdims=True)
    spread = jnp.mean(center * center, -1, keepdims=True)
    scale = lax.rsqrt(spread + 1e-05)
    unit = center * scale
    pulled = grad * gain
    first = jnp.mean(pulled, -1, keepdims=True)
    second = jnp.mean(pulled * unit, -1, keepdims=True)
    return (scale * (pulled - first - unit * second), jnp.sum(grad * unit, 0), jnp.sum(grad, 0))


def dot(left, right, dims):
    return lax.dot_general(left, right, (dims, ((), ())), preferred_element_type=F32)


def attention(triple, segment_all, grad_of):
    length = triple.shape[0]
    group = triple.shape[1] // (3 * HEAD_DIM)
    heads = triple.reshape(length, 3, group, HEAD_DIM)
    query, keys, values = (heads[:, 0], heads[:, 1], heads[:, 2])
    places = jnp.arange(length, dtype=jnp.int32)
    allowed = (segment_all[:, None] == segment_all[None, :]) & (places[None, :] <= places[:, None])
    scores = jnp.einsum("qhd,khd->hqk", query, keys, preferred_element_type=F32) * 0.125
    scores = jnp.where(allowed[None], scores, -jnp.inf)
    row_max = jnp.max(scores, -1, keepdims=True)
    expo = jnp.exp(scores - row_max)
    totals = jnp.sum(expo, -1, keepdims=True)
    probs = expo / totals
    probs_low = probs.astype(BF16)
    attended = jnp.einsum("hqk,khd->qhd", probs_low, values, preferred_element_type=F32)
    attended = attended.astype(BF16).reshape(length, -1)

    def pull(grad):
        grad = grad.reshape(length, group, HEAD_DIM)
        grad_probs = jnp.einsum("qhd,khd->hqk", grad, values, preferred_element_type=F32)
        inner_sum = jnp.sum(probs * grad_probs, -1, keepdims=True)
        grad_scores = (probs * (grad_probs - inner_sum)).astype(BF16)
        grad_query = (
            jnp.einsum("hqk,khd->qhd", grad_scores, keys, preferred_element_type=F32) * 0.125
        )
        grad_keys = (
            jnp.einsum("hqk,qhd->khd", grad_scores, query, preferred_element_type=F32) * 0.125
        )
        grad_values = jnp.einsum("hqk,qhd->khd", probs_low, grad, preferred_element_type=F32)
        stacked = jnp.stack([grad_query, grad_keys, grad_values], 1)
        return stacked.astype(BF16).reshape(length, -1)

    return (attended, pull)


def on_device(
    tokens,
    segments,
    qkv_weight,
    out_weight,
    up_weight,
    up_bias,
    down_weight,
    first_gain,
    first_shift,
    second_gain,
    second_shift,
    third_gain,
    third_shift,
    fourth_gain,
    fourth_shift,
    out_cotangent,
):
    n_seq = lax.axis_size("seq")
    n_fsdp = lax.axis_size("fsdp")
    width = tokens.shape[2]

    def columns(weight, parts):
        rows = weight.shape[0]
        cut = weight.reshape(rows, parts, n_seq, -1).transpose(2, 0, 1, 3).reshape(n_seq, rows, -1)
        cut = lax.all_to_all(cut, "seq", split_axis=0, concat_axis=0, tiled=True)
        whole = lax.all_gather(cut, "fsdp", axis=1, tiled=True)
        return whole.reshape(n_seq * n_fsdp * rows, -1)

    def columns_back(grad, parts):
        rows = grad.shape[0] // (n_seq * n_fsdp)
        cut = grad.astype(BF16).reshape(n_seq, n_fsdp, rows, -1).transpose(1, 0, 2, 3)
        cut = lax.psum_scatter(cut, "fsdp", scatter_dimension=0, tiled=True)[0]
        cut = lax.all_to_all(cut, "seq", split_axis=0, concat_axis=0, tiled=True)
        cut = cut.reshape(n_seq, rows, parts, -1).transpose(1, 2, 0, 3)
        return cut.reshape(rows, -1).astype(F32)

    def rows_back(grad):
        return lax.psum_scatter(grad.astype(BF16), "fsdp", scatter_dimension=0, tiled=True).astype(
            F32
        )

    def spread_rows(value):
        return lax.all_gather(value, "seq", axis=0, tiled=True)

    def sum_rows(value):
        return lax.psum_scatter(value.astype(BF16), "seq", scatter_dimension=0, tiled=True).astype(
            F32
        )

    segment_all = lax.all_gather(segments[0], "seq", axis=0, tiled=True)
    small = jnp.stack(
        [
            first_gain,
            first_shift,
            second_gain,
            second_shift,
            third_gain,
            third_shift,
            fourth_gain,
            fourth_shift,
        ]
    )
    small = lax.all_gather(small, ("seq", "fsdp"), axis=1, tiled=True).astype(F32)
    gain_a, shift_a, gain_b, shift_b, gain_c, shift_c, gain_d, shift_d = small
    qkv_w = columns(qkv_weight, 3)
    out_w = lax.all_gather(out_weight, "fsdp", axis=0, tiled=True)
    up_w = columns(up_weight, 1)
    up_b = lax.all_gather(up_bias, "fsdp", axis=0, tiled=True).astype(F32)
    down_w = lax.all_gather(down_weight, "fsdp", axis=0, tiled=True)
    inputs = tokens[0].astype(F32)
    cotangent = out_cotangent[0].astype(F32)
    normed = spread_rows(layer_norm(inputs, gain_a, shift_a).astype(BF16))
    triple = dot(normed, qkv_w, ((1,), (0,))).astype(BF16)
    attended, attend_pull = attention(triple, segment_all, None)
    branch = sum_rows(dot(attended, out_w, ((1,), (0,))))
    middle = inputs + layer_norm(branch, gain_b, shift_b)
    inner = spread_rows(layer_norm(middle, gain_c, shift_c).astype(BF16))
    pre = dot(inner, up_w, ((1,), (0,))) + up_b
    activ = jax.nn.gelu(pre, approximate=True).astype(BF16)
    mixed = sum_rows(dot(activ, down_w, ((1,), (0,))))
    result = middle + layer_norm(mixed, gain_d, shift_d)
    grad_mixed, grad_gain_d, grad_shift_d = norm_pull(mixed, gain_d, cotangent)
    grad_mixed = spread_rows(grad_mixed.astype(BF16))
    grad_activ = dot(grad_mixed, down_w, ((1,), (1,)))
    _, gelu_pull = jax.vjp(partial(jax.nn.gelu, approximate=True), pre)
    grad_pre = gelu_pull(grad_activ)[0].astype(BF16)
    grad_upbias = jnp.sum(grad_pre.astype(F32), 0)
    grad_inner = sum_rows(dot(grad_pre, up_w, ((1,), (1,))))
    grad_down = dot(activ, grad_mixed, ((0,), (0,)))
    grad_up = dot(inner, grad_pre, ((0,), (0,)))
    grad_side, grad_gain_c, grad_shift_c = norm_pull(middle, gain_c, grad_inner)
    grad_middle = cotangent + grad_side
    grad_branch, grad_gain_b, grad_shift_b = norm_pull(branch, gain_b, grad_middle)
    grad_branch = spread_rows(grad_branch.astype(BF16))
    grad_out = dot(attended, grad_branch, ((0,), (0,)))
    grad_attended = dot(grad_branch, out_w, ((1,), (1,))).astype(BF16)
    grad_triple = attend_pull(grad_attended)
    grad_qkv = dot(normed, grad_triple, ((0,), (0,)))
    grad_normed = sum_rows(dot(grad_triple, qkv_w, ((1,), (1,))))
    grad_first, grad_gain_a, grad_shift_a = norm_pull(inputs, gain_a, grad_normed)
    grad_inputs = grad_middle + grad_first
    small_grads = jnp.stack(
        [
            grad_gain_a,
            grad_shift_a,
            grad_gain_b,
            grad_shift_b,
            grad_gain_c,
            grad_shift_c,
            grad_gain_d,
            grad_shift_d,
        ]
    )
    small_grads = lax.psum_scatter(small_grads, ("seq", "fsdp"), scatter_dimension=1, tiled=True)
    grad_upbias = lax.psum_scatter(grad_upbias, "fsdp", scatter_dimension=0, tiled=True)
    return (
        result.astype(BF16)[None],
        grad_inputs[None],
        columns_back(grad_qkv, 3),
        rows_back(grad_out),
        columns_back(grad_up, 1),
        grad_upbias,
        rows_back(grad_down),
        small_grads[0],
        small_grads[1],
        small_grads[2],
        small_grads[3],
        small_grads[4],
        small_grads[5],
        small_grads[6],
        small_grads[7],
    )


def solution(mesh):
    rows = P(("seq", "fsdp"), None)
    vector = P(("seq", "fsdp"))
    acts = P("fsdp", "seq", None)
    placed = (acts, P("fsdp", "seq"), rows, rows, rows, vector, rows) + (vector,) * 8 + (acts,)
    return jax.shard_map(
        on_device,
        mesh=mesh,
        in_specs=placed,
        out_specs=(acts, acts, rows, rows, rows, vector, rows) + (vector,) * 8,
        check_vma=False,
    )
```

profile of v0, /device:TPU:0, one launch (start us, length us, event | category | flops | bytes accessed | tf_op | source)
XLA Modules:
  0.0 792.2 jit_solution(1543437263982148895)
XLA Ops:
  8.6 10.6 %all_to_all.20 = bf16[4,32,768]{2,1,0:T(8,128)(2,1)} all-to-all(bf16[4,32,768]{2,1,0:T(8,128)(2,1)S(1)} %reshape.212), channel_id=1, replica_groups=mesh['seq'=4,'fsdp'=8] {'seq'}, dimensions={0} | all-to-all | bytes 393216 | tf_op jit(solution)/shard_map/all_to_all | solution.py:93
  20.1 40.2 %all-gather.1 = bf16[32,32,8]{1,2,0:T(8,128)(2,1)S(1)} all-gather(bf16[1,32,8]{1,2,0:T(8,128)(2,1)S(1)} %bitcast.285), channel_id=1, replica_groups=mesh['seq'=4,'fsdp'=8] {'seq','fsdp'}, dimensions={0}, use_global_device_ids=true | all-gather | bytes 16896 | tf_op jit(solution)/shard_map/all_gather | solution.py:131
  63.0 2.1 fusion.70
  65.2 8.2 %all-gather = s32[1,1024]{1,0:T(1,128)S(1)} all-gather(s32[1,256]{1,0:T(1,128)S(1)} %copy-done.13), channel_id=2, replica_groups=mesh['seq'=4,'fsdp'=8] {'seq'}, dimensions={1}, use_global_device_ids=true | all-gather | bytes 5120 | tf_op jit(solution)/shard_map/all_gather | solution.py:118
  73.4 14.9 %all_gather.37 = bf16[256,1024]{1,0:T(8,128)(2,1)S(1)} all-gather(bf16[32,1024]{1,0:T(8,128)(2,1)S(1)} %copy-done.12), channel_id=1, replica_groups=mesh['seq'=4,'fsdp'=8] {'fsdp'}, dimensions={0}, use_global_device_ids=true | all-gather | bytes 589824 | tf_op jit(solution)/shard_map/all_gather | solution.py:134
  89.0 9.1 %all-gather.11.cloned.1.call-done = bf16[1024,1024]{1,0:T(8,128)(2,1)} async-done(((bf16[256,1024]{1,0:T(8,128)(2,1)}), bf16[1024,1024]{1,0:T(8,128)(2,1)}) %all-gather.11.cloned.1.call-update) | async-done | bytes 2097168 | tf_op jit(solution)/shard_map/all_gather | solution.py:111
  98.0 5.0 convolution_convert_fusion.7
  103.0 10.8 %fusion.94 = (f32[4,1024]{1,0:T(4,128)S(1)}, f32[4,1024,1024]{1,2,0:T(8,128)}) fusion(pred[1024,1024]{0,1:T(8,128)(4,1)S(1)} %fusion.16, bf16[1024,3,4,64]{0,3,2,1:T(8,128)(2,1)} %bitcast.243), kind=kOutput, calls=%fused_computation.151 | convolution fusion | flops 553649152 | bytes 18890752 | tf_op jit(solution)/shard_map/sub | solution.py:43
  113.8 7.5 fusion.38
  124.6 8.4 %all_to_all.21 = bf16[4,32,1024]{2,1,0:T(8,128)(2,1)S(1)} all-to-all(bf16[4,32,1024]{2,1,0:T(8,128)(2,1)S(1)} %copy.69), channel_id=1, replica_groups=mesh['seq'=4,'fsdp'=8] {'seq'}, dimensions={0} | all-to-all | bytes 524288 | tf_op jit(solution)/shard_map/all_to_all | solution.py:93
  134.1 25.5 %reduce-scatter.14.cloned.1.call-done = bf16[256,1024]{1,0:T(8,128)(2,1)} async-done(((bf16[1024,1024]{1,0:T(8,128)(2,1)}), bf16[256,1024]{1,0:T(8,128)(2,1)}) %reduce-scatter.14.cloned.1.call-update) | async-done | bytes 524304 | tf_op jit(solution)/shard_map/reduce_scatter | solution.py:114
  165.2 2.6 add_convert_fusion
  168.5 11.8 %all-gather.2 = bf16[8,1,128]{2,1,0:T(2,128)(2,1)S(1)} all-gather(bf16[1,1,128]{2,1,0:T(2,128)(2,1)S(1)} %bitcast.297), channel_id=1, replica_groups=mesh['seq'=4,'fsdp'=8] {'fsdp'}, dimensions={0}, use_global_device_ids=true | all-gather | bytes 2304 | tf_op jit(solution)/shard_map/all_gather | solution.py:136
  180.3 10.6 %all-gather.17.cloned.1.call-done = bf16[4,256,1024]{2,0,1:T(4,128)(2,1)} async-done(((bf16[4,32,1024]{2,0,1:T(4,128)(2,1)}), bf16[4,256,1024]{2,0,1:T(4,128)(2,1)}) %all-gather.17.cloned.1.call-update) | async-done | bytes 2097168 | tf_op jit(solution)/shard_map/all_gather | solution.py:94
  190.9 2.2 copy.71
  193.1 35.0 %all-gather.15.cloned.1.call-done = bf16[1024,1024]{1,0:T(8,128)(2,1)} async-done(((bf16[256,1024]{1,0:T(8,128)(2,1)}), bf16[1024,1024]{1,0:T(8,128)(2,1)}) %all-gather.15.cloned.1.call-update) | async-done | bytes 2097168 | tf_op jit(solution)/shard_map/all_gather | solution.py:111
  228.1 5.8 fusion.95
  234.0 24.8 %all-gather.19.cloned.1.call-done = bf16[1024,1024]{1,0:T(8,128)(2,1)} async-done(((bf16[128,1024]{1,0:T(8,128)(2,1)}), bf16[1024,1024]{1,0:T(8,128)(2,1)}) %all-gather.19.cloned.1.call-update) | async-done | bytes 2097168 | tf_op jit(solution)/shard_map/all_gather | solution.py:137
  258.8 7.1 convolution_convert_fusion.3
  265.9 34.8 %reduce-scatter.16.cloned.1.call-done = bf16[256,1024]{1,0:T(8,128)(2,1)} async-done(((bf16[1024,1024]{1,0:T(8,128)(2,1)}), bf16[256,1024]{1,0:T(8,128)(2,1)}) %reduce-scatter.16.cloned.1.call-update) | async-done | bytes 524304 | tf_op jit(solution)/shard_map/reduce_scatter | solution.py:114
  304.9 2.2 fusion.60
  307.4 35.2 %all-gather.21.cloned.1.call-done = bf16[1024,1024]{1,0:T(8,128)(2,1)} async-done(((bf16[256,1024]{1,0:T(8,128)(2,1)}), bf16[1024,1024]{1,0:T(8,128)(2,1)}) %all-gather.21.cloned.1.call-update) | async-done | bytes 2097168 | tf_op jit(solution)/shard_map/all_gather | solution.py:111
  342.6 7.3 convert_reduce_fusion
  351.2 5.4 convolution_convert_fusion.2
  356.7 35.3 %reduce-scatter.18.cloned.1.call-done = bf16[256,1024]{1,0:T(8,128)(2,1)} async-done(((bf16[1024,1024]{1,0:T(8,128)(2,1)}), bf16[256,1024]{1,0:T(8,128)(2,1)}) %reduce-scatter.18.cloned.1.call-update) | async-done | bytes 524304 | tf_op jit(solution)/shard_map/reduce_scatter | solution.py:114
  393.9 3.4 fusion.67
  398.5 6.0 convolution_convert_fusion.1
  405.0 28.9 %all-gather.23.cloned.1.call-done = bf16[1024,1024]{1,0:T(8,128)(2,1)} async-done(((bf16[256,1024]{1,0:T(8,128)(2,1)}), bf16[1024,1024]{1,0:T(8,128)(2,1)}) %all-gather.23.cloned.1.call-update) | async-done | bytes 2097168 | tf_op jit(solution)/shard_map/all_gather | solution.py:111
  433.9 2.5 convolution_convert_fusion.9
  437.2 9.6 %fusion.25 = bf16[1024,1,4,64]{0,3,2,1:T(8,128)(2,1)} fusion(bf16[1024,4,64]{0,2,1:T(8,128)(2,1)S(1)} %bitcast.308, f32[4,1024,1024]{1,2,0:T(8,128)} %get-tuple-element.51, f32[4,1024]{1,0:T(4,128)S(1)} %get-tuple-element.50), kind=kOutput, calls=%fused_computation.50 | convolution fusion | flops 545259520 | bytes 17842176 | tf_op jit(solution)/shard_map/hqk,qhd->khd/dot_general | solution.py:61
  446.9 9.4 %multiply_reduce_fusion = (f32[4,1024]{1,0:T(4,128)S(1)}, f32[4,1024,1024]{1,2,0:T(8,128)}) fusion(f32[4,1024,1024]{1,2,0:T(8,128)S(1)} %bitcast.229, f32[4,1024]{1,0:T(4,128)S(1)} %get-tuple-element.50, bf16[1024,4,64]{0,2,1:T(8,128)(2,1)} %bitcast.309, bf16[1024,3,4,64]{0,3,2,1:T(8,128)(2,1)} %bitcast.245), kind=kOutput, calls=%fused_computation.2 | convolution fusion | flops 549449728 | bytes 34635776 | tf_op jit(solution)/shard_map/qhd,khd->hqk/dot_general | solution.py:52
  456.3 7.9 %multiply_convert_fusion = bf16[4,1024,1024]{1,2,0:T(8,128)(2,1)S(1)} fusion(f32[4,1024,1024]{1,2,0:T(8,128)} %get-tuple-element.53, f32[4,1024]{1,0:T(4,128)S(1)} %get-tuple-element.52, f32[4,1024,1024]{1,2,0:T(8,128)S(1)} %bitcast.229, f32[4,1024]{1,0:T(4,128)S(1)} %get-tuple-element.50), kind=kLoop, calls=%fused_computation.1 | loop fusion | flops 16777216 | bytes 41975808 | tf_op jit(solution)/shard_map/convert_element_type | solution.py:54
  464.2 3.7 fusion.28
  467.9 2.8 fusion.29
  474.4 7.4 convolution_convert_fusion
  481.8 3.1 convolution_convert_fusion.8
  485.0 5.1 convolution_convert_fusion.5
  490.8 10.7 %all-reduce.4.cloned.1.call-done = bf16[8,4,32,1024]{3,2,0,1:T(8,128)(2,1)} async-done(((bf16[8,4,32,1024]{3,2,0,1:T(8,128)(2,1)}), bf16[8,4,32,1024]{3,2,0,1:T(8,128)(2,1)}) %all-reduce.4.cloned.1.call-update) | async-done | bytes 2097168
  501.4 2.3 dynamic-slice_bitcast_fusion
  503.7 3.6 all-to-all-start.3
  508.1 13.7 %all-reduce.1 = f32[1024]{0:T(1024)S(1)} all-reduce(f32[1024]{0:T(1024)S(1)} %get-tuple-element.30), channel_id=10, replica_groups=mesh['seq'=4,'fsdp'=8] {'fsdp'}, use_global_device_ids=true, to_apply=%region_27.28.clone | all-reduce | flops 1024 | bytes 8192
  522.4 15.0 %reduce-scatter.22.cloned.1.call-done = bf16[1,4,32,768]{3,2,1,0:T(8,128)(2,1)} async-done(((bf16[8,4,32,768]{3,2,1,0:T(8,128)(2,1)}), bf16[1,4,32,768]{3,2,1,0:T(8,128)(2,1)}) %reduce-scatter.22.cloned.1.call-update) | async-done | bytes 196624 | tf_op jit(solution)/shard_map/reduce_scatter | solution.py:100
  537.4 4.0 all-to-all-start.2
  542.9 31.2 %reduce-scatter.26.cloned.1.call-done = bf16[128,1024]{1,0:T(8,128)(2,1)} async-done(((bf16[1024,1024]{1,0:T(8,128)(2,1)}), bf16[128,1024]{1,0:T(8,128)(2,1)}) %reduce-scatter.26.cloned.1.call-update) | async-done | bytes 262160 | tf_op jit(solution)/shard_map/reduce_scatter | solution.py:106
  576.0 30.6 %reduce-scatter.24.cloned.1.call-done = bf16[32,1024]{1,0:T(8,128)(2,1)} async-done(((bf16[256,1024]{1,0:T(8,128)(2,1)}), bf16[32,1024]{1,0:T(8,128)(2,1)}) %reduce-scatter.24.cloned.1.call-update) | async-done | bytes 65552 | tf_op jit(solution)/shard_map/reduce_scatter | solution.py:106
  609.5 33.3 %reduce-scatter.20.cloned.1.call-done = bf16[256,1024]{1,0:T(8,128)(2,1)} async-done(((bf16[1024,1024]{1,0:T(8,128)(2,1)}), bf16[256,1024]{1,0:T(8,128)(2,1)}) %reduce-scatter.20.cloned.1.call-update) | async-done | bytes 524304 | tf_op jit(solution)/shard_map/reduce_scatter | solution.py:114
  645.5 2.4 fusion.74
  647.9 131.7 %reduce-scatter.28.cloned.1.call-done = f32[32,8]{1,0:T(8,128)} async-done(((f32[1024,8]{1,0:T(8,128)}), f32[32,8]{1,0:T(8,128)}) %reduce-scatter.28.cloned.1.call-update) | async-done | bytes 1040
  (149 shorter events, 46.0 us)
Async XLA Ops:
  7.2 58.0 %copy-start.13 = (s32[1,256]{1,0:T(1,128)S(1)}, s32[1,256]{1,0:T(1,128)}, u32[]{:S(2)}) copy-start(s32[1,256]{1,0:T(1,128)} %param.17) | copy-start | bytes 3076
  7.2 66.2 %copy-start.12 = (bf16[32,1024]{1,0:T(8,128)(2,1)S(1)}, bf16[32,1024]{1,0:T(8,128)(2,1)}, u32[]{:S(2)}) copy-start(bf16[32,1024]{1,0:T(8,128)(2,1)} %param.19) | copy-start | bytes 196612
  7.2 81.8 %all-gather.13.cloned.1.call-start = ((), (), s32[]{:S(2)}) async-start(), calls=%async_computation.13 | async-start | bytes 1769472 | tf_op jit(solution)/shard_map/all_gather | solution.py:94
  19.3 78.7 %all-gather.11.cloned.1.call-start = ((), (), s32[]{:S(2)}) async-start(), calls=%async_computation.12 | async-start | bytes 2621440 | tf_op jit(solution)/shard_map/all_gather | solution.py:111
  65.2 94.4 %reduce-scatter.14.cloned.1.call-start = ((), (), s32[]{:S(2)}) async-start(), calls=%async_computation.14 | async-start | bytes 2621440 | tf_op jit(solution)/shard_map/reduce_scatter | solution.py:114
  88.3 33.0 %copy-start.5 = (bf16[256,1024]{1,0:T(8,128)(2,1)}, bf16[256,1024]{1,0:T(8,128)(2,1)S(1)}, u32[]{:S(2)}) copy-start(bf16[256,1024]{1,0:T(8,128)(2,1)S(1)} %all_gather.37) | copy-start | bytes 1572868
  121.4 0.8 copy-start.8
  121.4 2.9 copy-start.11
  122.2 40.0 %copy-start = (bf16[1,256,1024]{2,1,0:T(8,128)(2,1)S(1)}, bf16[1,256,1024]{2,1,0:T(8,128)(2,1)}, u32[]{:S(2)}) copy-start(bf16[1,256,1024]{2,1,0:T(8,128)(2,1)} %param.16) | copy-start | bytes 1572868
  124.2 44.2 %copy-start.14 = (bf16[128]{0:T(256)(128)(2,1)S(1)}, bf16[128]{0:T(256)(128)(2,1)}, u32[]{:S(2)}) copy-start(bf16[128]{0:T(256)(128)(2,1)} %param.21) | copy-start | bytes 772
  124.2 66.6 %all-gather.17.cloned.1.call-start = ((), (), s32[]{:S(2)}) async-start(), calls=%async_computation.16 | async-start | bytes 2359296 | tf_op jit(solution)/shard_map/all_gather | solution.py:94
  133.9 94.2 %all-gather.15.cloned.1.call-start = ((), (), s32[]{:S(2)}) async-start(), calls=%async_computation.15 | async-start | bytes 2621440 | tf_op jit(solution)/shard_map/all_gather | solution.py:111
  167.8 90.9 %all-gather.19.cloned.1.call-start = ((), (), s32[]{:S(2)}) async-start(), calls=%async_computation.17 | async-start | bytes 2359296 | tf_op jit(solution)/shard_map/all_gather | solution.py:137
  168.4 132.3 %reduce-scatter.16.cloned.1.call-start = ((), (), s32[]{:S(2)}) async-start(), calls=%async_computation.18 | async-start | bytes 2621440 | tf_op jit(solution)/shard_map/reduce_scatter | solution.py:114
  193.1 40.9 %copy-start.4 = (bf16[4,256,1024]{2,1,0:T(8,128)(2,1)}, bf16[4,256,1024]{2,1,0:T(8,128)(2,1)S(1)}, u32[]{:S(2)}) copy-start(bf16[4,256,1024]{2,1,0:T(8,128)(2,1)S(1)} %copy.71) | copy-start | bytes 6291460
  258.8 44.5 %copy-start.3 = (bf16[1,256,1024]{2,1,0:T(8,128)(2,1)S(1)}, bf16[1,256,1024]{2,1,0:T(8,128)(2,1)}, u32[]{:S(2)}) copy-start(bf16[1,256,1024]{2,1,0:T(8,128)(2,1)} %param.31) | copy-start | bytes 1572868
  265.8 76.7 %copy-start.16 = (bf16[1024,1024]{1,0:T(8,128)(2,1)S(1)}, bf16[1024,1024]{1,0:T(8,128)(2,1)}, u32[]{:S(2)}) copy-start(bf16[1024,1024]{1,0:T(8,128)(2,1)} %all-gather.19.cloned.1.call-done) | copy-start | bytes 6291460
  265.9 76.7 %all-gather.21.cloned.1.call-start = ((), (), s32[]{:S(2)}) async-start(), calls=%async_computation.19 | async-start | bytes 2621440 | tf_op jit(solution)/shard_map/all_gather | solution.py:111
  307.1 84.9 %reduce-scatter.18.cloned.1.call-start = ((), (), s32[]{:S(2)}) async-start(), calls=%async_computation.20 | async-start | bytes 2621440 | tf_op jit(solution)/shard_map/reduce_scatter | solution.py:114
  349.9 1.3 copy-start.19
  351.2 40.8 %copy-start.1 = (bf16[256,1024]{1,0:T(8,128)(2,1)S(1)}, bf16[256,1024]{1,0:T(8,128)(2,1)}, u32[]{:S(2)}) copy-start(bf16[256,1024]{1,0:T(8,128)(2,1)} %reduce-scatter.14.cloned.1.call-done) | copy-start | bytes 1572868
  351.2 42.7 %copy-start.2 = (bf16[256,1024]{1,0:T(8,128)(2,1)S(1)}, bf16[256,1024]{1,0:T(8,128)(2,1)}, u32[]{:S(2)}) copy-start(bf16[256,1024]{1,0:T(8,128)(2,1)} %reduce-scatter.16.cloned.1.call-done) | copy-start | bytes 1572868
  356.6 77.3 %all-gather.23.cloned.1.call-start = ((), (), s32[]{:S(2)}) async-start(), calls=%async_computation.21 | async-start | bytes 2621440 | tf_op jit(solution)/shard_map/all_gather | solution.py:111
  398.4 35.5 %copy-start.6 = (bf16[256,1024]{1,0:T(8,128)(2,1)S(1)}, bf16[256,1024]{1,0:T(8,128)(2,1)}, u32[]{:S(2)}) copy-start(bf16[256,1024]{1,0:T(8,128)(2,1)} %copy-done.5) | copy-start | bytes 1572868
  398.5 103.0 %all-reduce.4.cloned.1.call-start = ((), (), s32[]{:S(2)}) async-start(), calls=%async_computation.27 | async-start | bytes 4194304
  404.6 132.8 %reduce-scatter.22.cloned.1.call-start = ((), (), s32[]{:S(2)}) async-start(), calls=%async_computation.23 | async-start | bytes 1769472 | tf_op jit(solution)/shard_map/reduce_scatter | solution.py:100
  433.9 12.9 %slice-start = ((s8[16777216]{0:T(1024)(128)(4,1)}), s8[4194304]{0:T(1024)(128)(4,1)S(1)}, s32[]{:S(2)}) async-start(s8[16777216]{0:T(1024)(128)(4,1)} %bitcast.228), calls=%async_computation.28 | async-start | bytes 8388608
  436.4 0.8 copy-start.17
  437.2 9.6 %slice-start.1 = ((s8[16777216]{0:T(1024)(128)(4,1)}), s8[4194304]{0:T(1024)(128)(4,1)S(1)}, s32[]{:S(2)}) async-start(s8[16777216]{0:T(1024)(128)(4,1)} %bitcast.228), calls=%async_computation.29 | async-start | bytes 8388608
  437.2 9.6 %slice-start.2 = ((s8[16777216]{0:T(1024)(128)(4,1)}), s8[4194304]{0:T(1024)(128)(4,1)S(1)}, s32[]{:S(2)}) async-start(s8[16777216]{0:T(1024)(128)(4,1)} %bitcast.228), calls=%async_computation.30 | async-start | bytes 8388608
  437.2 9.7 %slice-start.3 = ((s8[16777216]{0:T(1024)(128)(4,1)}), s8[4194304]{0:T(1024)(128)(4,1)S(1)}, s32[]{:S(2)}) async-start(s8[16777216]{0:T(1024)(128)(4,1)} %bitcast.228), calls=%async_computation.31 | async-start | bytes 8388608
  467.9 2.8 copy-start.10
  467.9 3.0 copy-start.15
  470.9 1.9 copy-start.7
  474.1 7.7 copy-start.9
  474.2 100.0 %reduce-scatter.26.cloned.1.call-start = ((), (), s32[]{:S(2)}) async-start(), calls=%async_computation.25 | async-start | bytes 2359296 | tf_op jit(solution)/shard_map/reduce_scatter | solution.py:106
  481.8 124.8 %reduce-scatter.24.cloned.1.call-start = ((), (), s32[]{:S(2)}) async-start(), calls=%async_computation.24 | async-start | bytes 589824 | tf_op jit(solution)/shard_map/reduce_scatter | solution.py:106
  485.0 5.2 copy-start.18
  485.0 157.8 %reduce-scatter.20.cloned.1.call-start = ((), (), s32[]{:S(2)}) async-start(), calls=%async_computation.22 | async-start | bytes 2621440 | tf_op jit(solution)/shard_map/reduce_scatter | solution.py:114
  503.7 18.7 %all-to-all-start.3 = ((bf16[4,32,1024]{2,1,0:T(8,128)(2,1)}), bf16[4,32,1024]{2,1,0:T(8,128)(2,1)S(1)}, u32[]{:S(2)}, u32[]{:S(2)}) async-start(bf16[4,32,1024]{2,1,0:T(8,128)(2,1)} %dynamic-slice_bitcast_fusion), calls=%async_computation.9 | async-start | bytes 524288 | tf_op jit(solution)/shard_map/all_to_all | solution.py:101
  537.4 70.7 %all-to-all-start.2 = ((bf16[4,32,768]{2,1,0:T(8,128)(2,1)}), bf16[4,32,768]{2,1,0:T(8,128)(2,1)S(1)}, u32[]{:S(2)}, u32[]{:S(2)}) async-start(bf16[4,32,768]{2,1,0:T(8,128)(2,1)} %bitcast.257), calls=%async_computation.7 | async-start | bytes 393216 | tf_op jit(solution)/shard_map/all_to_all | solution.py:101
  541.4 238.2 %reduce-scatter.28.cloned.1.call-start = ((), (), s32[]{:S(2)}) async-start(), calls=%async_computation.26 | async-start | bytes 540672
Sparse Core Ops, SparseCore 0:
  19.4 24.8 all-gather.12
  65.3 32.6 all-gather.10
  124.4 35.1 reduce-scatter.13
  161.7 29.1 all-gather.16
  193.3 34.7 all-gather.14
  229.6 29.0 all-gather.18
  266.0 34.6 reduce-scatter.15
  307.2 35.2 all-gather.20
  356.8 35.1 reduce-scatter.17
  398.6 35.2 all-gather.22
  436.4 64.9 all-reduce.3
  503.7 33.6 reduce-scatter.21
  539.8 34.2 reduce-scatter.25
  577.0 29.5 reduce-scatter.23
  609.4 33.3 reduce-scatter.19
  645.7 133.9 reduce-scatter.27
where the time goes:
time: 802 us; the launch traced here: 792 us
  waiting for transfers between devices  493 us (61%)
  blocking collectives  108 us (13%)
  matrix products  102 us (13%)
  other arithmetic  41.7 us (5%)
  local copies, waits for them, and re-layouts  23.2 us (3%)
  between operations  15.3 us (2%)
  starting transfers between devices  9.24 us (1%)
    unnamed x18, waiting for transfers between devices  143 us
    reduce_scatter x4, waiting for transfers between devices, sum_rows(): lax.psum_scatter(value.astype(BF16), 'seq', scatter_dimension=0, tiled=True)  129 us
    all_gather x4, waiting for transfers between devices, spread_rows(): return lax.all_gather(value, 'seq', axis=0, tiled=True)  108 us
    reduce_scatter x2, waiting for transfers between devices, rows_back(): lax.psum_scatter(grad.astype(BF16), 'fsdp', scatter_dimension=0, tiled=True)  61.9 us
    dot_general x12, matrix products, dot(): lax.dot_general(left, right, (dims, ((), ())), preferred_element_type=F32)  58.7 us
    all_gather x1, blocking collectives, on_device(): lax.all_gather(small, ('seq', 'fsdp'), axis=1, tiled=True).astype(F32)  40.2 us
    all_gather x1, waiting for transfers between devices, on_device(): down_w = lax.all_gather(down_weight, 'fsdp', axis=0, tiled=True)  24.8 us
    all_to_all x2, blocking collectives, columns(): cut = lax.all_to_all(cut, 'seq', split_axis=0, concat_axis=0, tiled=True)  19 us
  transfers between devices with their start and end apart: 18, of which 15 were waited for; matrix products, arithmetic and copies ran while one was open for 12% of the time, Pallas kernels for 0%

commit v1 on v0

--- a/solution.py
+++ b/solution.py
@@ -1,3 +1,4 @@
+import functools
 from functools import partial
 import jax
 import jax.numpy as jnp
@@ -7,6 +8,33 @@
 HEAD_DIM = 64
 F32 = jnp.float32
 BF16 = jnp.bfloat16
+
+
+def tell_keys(content, ndim_at):
+    content = jnp.moveaxis(content, 0, ndim_at)
+    near = content.shape
+    return content.reshape(*near[:ndim_at], near[ndim_at] * near[ndim_at + 1], *near[ndim_at + 2 :])
+
+
+def screen_clear(inp, axis_key):
+    parts_n = lax.axis_size(axis_key)
+    big = inp[None]
+    for dev_j in range(parts_n.bit_length() - 1):
+        arr_out = 1 << dev_j
+        even = lax.ppermute(
+            big, axis_name=axis_key, perm=[(u, u ^ arr_out) for u in range(parts_n)]
+        )
+        aux = jnp.stack([big, even])
+        found_now = lax.axis_index(axis_key) >> dev_j & 1
+        big = jnp.where(found_now == 0, aux, aux[::-1]).reshape(-1, *inp.shape)
+    return big
+
+
+def show_the_case(my_tile, w_in, array_dim):
+    return tell_keys(screen_clear(my_tile, w_in), array_dim)
+
+
+part_record = functools.partial(show_the_case, w_in="seq", array_dim=0)
 
 
 def layer_norm(value, gain, shift):
@@ -108,7 +136,7 @@
         )
 
     def spread_rows(value):
-        return lax.all_gather(value, "seq", axis=0, tiled=True)
+        return part_record(value)
 
     def sum_rows(value):
         return lax.psum_scatter(value.astype(BF16), "seq", scatter_dimension=0, tiled=True).astype(

time: 802 us -> 768 us (0.958)
  waiting for transfers between devices: 493 us -> 425 us
  blocking collectives: 108 us -> 122 us
  starting transfers between devices: 9.24 us -> 23.2 us
  matrix products: 102 us -> 91.6 us
  local copies, waits for them, and re-layouts: 23.2 us -> 31.4 us
    all_gather x4 -> x0, waiting for transfers between devices: 108 us -> none  [spread_rows(): return lax.all_gather(value, 'seq', axis=0, tiled=True)]
    ppermute x0 -> x8, waiting for transfers between devices: none -> 99.5 us  [screen_clear(): lax.ppermute(big, axis_name=axis_key, perm=[(u, u ^ arr_out) for u in ran...]
    all_gather x1, blocking collectives: 8.18 us -> 26.4 us  [on_device(): segment_all = lax.all_gather(segments[0], 'seq', axis=0, tiled=True)]
    reduce_scatter x1, waiting for transfers between devices: 15 us -> 0.01 us  [columns_back(): cut = lax.psum_scatter(cut, 'fsdp', scatter_dimension=0, tiled=True)[0]]
    all_gather x1, waiting for transfers between devices: 24.8 us -> 10.1 us  [on_device(): down_w = lax.all_gather(down_weight, 'fsdp', axis=0, tiled=True)]
    all_gather x2, waiting for transfers between devices: 10.6 us -> 0.02 us  [columns(): whole = lax.all_gather(cut, 'fsdp', axis=1, tiled=True)]
    unnamed x18 -> x14, waiting for transfers between devices: 143 us -> 133 us
    ppermute x0 -> x8, starting transfers between devices: none -> 9.52 us  [screen_clear(): lax.ppermute(big, axis_name=axis_key, perm=[(u, u ^ arr_out) for u in ran...]
  transfers between devices with their start and end apart: 18 -> 23, of which waited for: 15 -> 15; matrix products, arithmetic and copies ran while one was open for 12% -> 12% of each run, Pallas kernels for 0% -> 0%
where the time goes in v1:
time: 768 us; the launch traced here: 758 us
  waiting for transfers between devices  425 us (55%)
  blocking collectives  122 us (16%)
  matrix products  91.6 us (12%)
  other arithmetic  48.6 us (6%)
  local copies, waits for them, and re-layouts  31.4 us (4%)
  starting transfers between devices  23.2 us (3%)
  between operations  15.9 us (2%)
    unnamed x14, waiting for transfers between devices  133 us
    reduce_scatter x4, waiting for transfers between devices, sum_rows(): lax.psum_scatter(value.astype(BF16), 'seq', scatter_dimension=0, tiled=True)  123 us
    ppermute x8, waiting for transfers between devices, screen_clear(): lax.ppermute(big, axis_name=axis_key, perm=[(u, u ^ arr_out) for u in ran...  99.5 us
    reduce_scatter x2, waiting for transfers between devices, rows_back(): lax.psum_scatter(grad.astype(BF16), 'fsdp', scatter_dimension=0, tiled=True)  59.6 us
    dot_general x12, matrix products, dot(): lax.dot_general(left, right, (dims, ((), ())), preferred_element_type=F32)  49.3 us
    all_gather x1, blocking collectives, on_device(): lax.all_gather(small, ('seq', 'fsdp'), axis=1, tiled=True).astype(F32)  42.5 us
    all_gather x1, blocking collectives, on_device(): segment_all = lax.all_gather(segments[0], 'seq', axis=0, tiled=True)  26.4 us
    unnamed x100, local copies, waits for them, and re-layouts  19.2 us
  transfers between devices with their start and end apart: 23, of which 15 were waited for; matrix products, arithmetic and copies ran while one was open for 12% of the time, Pallas kernels for 0%

profile of v1, /device:TPU:0, one launch (start us, length us, event | category | flops | bytes accessed | tf_op | source)
XLA Modules:
  0.0 757.9 jit_solution(2444941821536806892)
XLA Ops:
  9.4 5.2 all-to-all-start
  15.9 42.5 %all-gather.1 = bf16[32,32,8]{1,2,0:T(8,128)(2,1)S(1)} all-gather(bf16[1,32,8]{1,2,0:T(8,128)(2,1)S(1)} %bitcast.372), channel_id=1, replica_groups=mesh['seq'=4,'fsdp'=8] {'seq','fsdp'}, dimensions={0}, use_global_device_ids=true | all-gather | bytes 16896 | tf_op jit(solution)/shard_map/all_gather | solution.py:159
  60.3 13.9 %collective-permute-done = bf16[1,256,1024]{2,1,0:T(8,128)(2,1)S(1)} collective-permute-done((bf16[1,256,1024]{2,1,0:T(8,128)(2,1)S(1)}, bf16[1,256,1024]{2,1,0:T(8,128)(2,1)S(1)}, u32[]{:S(2)}, u32[]{:S(2)}) %collective-permute-start) | collective-permute-done | bytes 524320 | tf_op jit(solution)/shard_map/ppermute | solution.py:24
  75.4 26.4 %all-gather = s32[1,1024]{1,0:T(1,128)S(1)} all-gather(s32[1,256]{1,0:T(1,128)S(1)} %copy-done.29), channel_id=2, replica_groups=mesh['seq'=4,'fsdp'=8] {'seq'}, dimensions={1}, use_global_device_ids=true | all-gather | bytes 5120 | tf_op jit(solution)/shard_map/all_gather | solution.py:146
  101.8 15.0 %all_gather.24 = bf16[256,1024]{1,0:T(8,128)(2,1)S(1)} all-gather(bf16[32,1024]{1,0:T(8,128)(2,1)S(1)} %copy-done.24), channel_id=1, replica_groups=mesh['seq'=4,'fsdp'=8] {'fsdp'}, dimensions={0}, use_global_device_ids=true | all-gather | bytes 589824 | tf_op jit(solution)/shard_map/all_gather | solution.py:162
  120.4 5.2 convolution_convert_fusion.7
  125.7 11.1 %fusion.114 = (f32[4,1024]{1,0:T(4,128)S(1)}, f32[4,1024,1024]{1,2,0:T(8,128)}) fusion(pred[1024,1024]{0,1:T(8,128)(4,1)} %fusion.16, bf16[1024,3,4,64]{0,3,2,1:T(8,128)(2,1)} %bitcast.318), kind=kOutput, calls=%fused_computation.187 | convolution fusion | flops 553649152 | bytes 18890752 | tf_op jit(solution)/shard_map/sub | solution.py:71
  136.8 7.5 fusion.33
  145.1 2.1 convolution_convert_fusion.4
  147.6 11.4 %all_to_all.20 = bf16[4,32,1024]{2,1,0:T(8,128)(2,1)S(1)} all-to-all(bf16[4,32,1024]{2,1,0:T(8,128)(2,1)S(1)} %copy.87), channel_id=1, replica_groups=mesh['seq'=4,'fsdp'=8] {'seq'}, dimensions={0} | all-to-all | bytes 524288 | tf_op jit(solution)/shard_map/all_to_all | solution.py:121
  160.6 19.5 %reduce-scatter.14.cloned.1.call-done = bf16[256,1024]{1,0:T(8,128)(2,1)} async-done(((bf16[1024,1024]{1,0:T(8,128)(2,1)}), bf16[256,1024]{1,0:T(8,128)(2,1)}) %reduce-scatter.14.cloned.1.call-update) | async-done | bytes 524304 | tf_op jit(solution)/shard_map/reduce_scatter | solution.py:142
  187.2 11.8 %collective-permute-done.2 = bf16[1,256,1024]{2,1,0:T(8,128)(2,1)S(1)} collective-permute-done((bf16[1,256,1024]{2,1,0:T(8,128)(2,1)S(1)}, bf16[1,256,1024]{2,1,0:T(8,128)(2,1)S(1)}, u32[]{:S(2)}, u32[]{:S(2)}) %collective-permute-start.2) | collective-permute-done | bytes 524320 | tf_op jit(solution)/shard_map/ppermute | solution.py:24
  201.0 11.7 %all-gather.2 = bf16[8,1,128]{2,1,0:T(2,128)(2,1)S(1)} all-gather(bf16[1,1,128]{2,1,0:T(2,128)(2,1)S(1)} %bitcast.384), channel_id=1, replica_groups=mesh['seq'=4,'fsdp'=8] {'fsdp'}, dimensions={0}, use_global_device_ids=true | all-gather | bytes 2304 | tf_op jit(solution)/shard_map/all_gather | solution.py:164
  212.7 2.2 copy.89
  215.0 8.8 %collective-permute-done.3 = bf16[2,256,1024]{2,1,0:T(8,128)(2,1)} collective-permute-done((bf16[2,256,1024]{2,1,0:T(8,128)(2,1)S(1)}, bf16[2,256,1024]{2,1,0:T(8,128)(2,1)}, u32[]{:S(2)}, u32[]{:S(2)}) %collective-permute-start.3) | collective-permute-done | bytes 1048608 | tf_op jit(solution)/shard_map/ppermute | solution.py:24
  227.2 4.4 fusion.115
  231.5 10.1 %all-gather.11.cloned.1.call-done = bf16[1024,1024]{1,0:T(8,128)(2,1)} async-done(((bf16[128,1024]{1,0:T(8,128)(2,1)}), bf16[1024,1024]{1,0:T(8,128)(2,1)}) %all-gather.11.cloned.1.call-update) | async-done | bytes 2097168 | tf_op jit(solution)/shard_map/all_gather | solution.py:165
  241.7 7.0 convolution_convert_fusion.3
  249.0 34.6 %reduce-scatter.16.cloned.1.call-done = bf16[256,1024]{1,0:T(8,128)(2,1)} async-done(((bf16[1024,1024]{1,0:T(8,128)(2,1)}), bf16[256,1024]{1,0:T(8,128)(2,1)}) %reduce-scatter.16.cloned.1.call-update) | async-done | bytes 524304 | tf_op jit(solution)/shard_map/reduce_scatter | solution.py:142
  290.1 11.9 %collective-permute-done.4 = bf16[1,256,1024]{2,1,0:T(8,128)(2,1)S(1)} collective-permute-done((bf16[1,256,1024]{2,1,0:T(8,128)(2,1)S(1)}, bf16[1,256,1024]{2,1,0:T(8,128)(2,1)S(1)}, u32[]{:S(2)}, u32[]{:S(2)}) %collective-permute-start.4) | collective-permute-done | bytes 524320 | tf_op jit(solution)/shard_map/ppermute | solution.py:24
  303.8 22.6 %collective-permute-done.5 = bf16[2,256,1024]{2,1,0:T(8,128)(2,1)S(1)} collective-permute-done((bf16[2,256,1024]{2,1,0:T(8,128)(2,1)S(1)}, bf16[2,256,1024]{2,1,0:T(8,128)(2,1)S(1)}, u32[]{:S(2)}, u32[]{:S(2)}) %collective-permute-start.5) | collective-permute-done | bytes 1048608 | tf_op jit(solution)/shard_map/ppermute | solution.py:24
  327.2 2.1 copy-done.41
  330.1 5.1 convert_reduce_fusion
  336.5 3.7 convolution_convert_fusion.2
  340.3 35.3 %reduce-scatter.18.cloned.1.call-done = bf16[256,1024]{1,0:T(8,128)(2,1)} async-done(((bf16[1024,1024]{1,0:T(8,128)(2,1)}), bf16[256,1024]{1,0:T(8,128)(2,1)}) %reduce-scatter.18.cloned.1.call-update) | async-done | bytes 524304 | tf_op jit(solution)/shard_map/reduce_scatter | solution.py:142
  375.6 1.9 fusion.84
  377.5 3.4 fusion.76
  383.1 11.9 %collective-permute-done.6 = bf16[1,256,1024]{2,1,0:T(8,128)(2,1)S(1)} collective-permute-done((bf16[1,256,1024]{2,1,0:T(8,128)(2,1)S(1)}, bf16[1,256,1024]{2,1,0:T(8,128)(2,1)S(1)}, u32[]{:S(2)}, u32[]{:S(2)}) %collective-permute-start.6) | collective-permute-done | bytes 524320 | tf_op jit(solution)/shard_map/ppermute | solution.py:24
  398.2 3.7 convolution_convert_fusion.1
  402.4 18.7 %collective-permute-done.7 = bf16[2,256,1024]{2,1,0:T(8,128)(2,1)} collective-permute-done((bf16[2,256,1024]{2,1,0:T(8,128)(2,1)}, bf16[2,256,1024]{2,1,0:T(8,128)(2,1)}, u32[]{:S(2)}, u32[]{:S(2)}) %collective-permute-start.7) | collective-permute-done | bytes 1048608 | tf_op jit(solution)/shard_map/ppermute | solution.py:24
  424.5 8.7 %fusion.54 = bf16[1024,1,4,64]{0,3,2,1:T(8,128)(2,1)S(1)} fusion(bf16[1024,4,64]{0,2,1:T(8,128)(2,1)S(1)} %bitcast.395, f32[4,1024,1024]{1,2,0:T(8,128)} %get-tuple-element.59, f32[4,1024]{1,0:T(4,128)S(1)} %get-tuple-element.58), kind=kOutput, calls=%fused_computation.101 | convolution fusion | flops 545521664 | bytes 17842176 | tf_op jit(solution)/shard_map/hqk,qhd->khd/dot_general | solution.py:89
  433.2 10.7 %multiply_reduce_fusion = (f32[4,1024]{1,0:T(4,128)S(1)}, f32[4,1024,1024]{1,2,0:T(8,128)}) fusion(f32[4,1024,1024]{1,2,0:T(8,128)} %get-tuple-element.59, f32[4,1024]{1,0:T(4,128)S(1)} %get-tuple-element.58, bf16[1024,4,64]{0,2,1:T(8,128)(2,1)S(1)} %bitcast.396, bf16[1024,3,4,64]{0,3,2,1:T(8,128)(2,1)S(1)} %bitcast.320), kind=kOutput, calls=%fused_computation.2 | convolution fusion | flops 549449728 | bytes 34635776 | tf_op jit(solution)/shard_map/qhd,khd->hqk/dot_general | solution.py:80
  443.9 11.9 %multiply_convert_fusion = bf16[4,1024,1024]{1,2,0:T(8,128)(2,1)S(1)} fusion(f32[4,1024,1024]{1,2,0:T(8,128)} %get-tuple-element.61, f32[4,1024]{1,0:T(4,128)S(1)} %get-tuple-element.60, f32[4,1024,1024]{1,2,0:T(8,128)} %get-tuple-element.59, f32[4,1024]{1,0:T(4,128)S(1)} %get-tuple-element.58), kind=kLoop, calls=%fused_computation.1 | loop fusion | flops 16777216 | bytes 41975808 | tf_op jit(solution)/shard_map/convert_element_type | solution.py:82
  455.7 2.7 fusion.57
  460.2 2.0 copy-done.6
  462.2 1.9 convolution_convert_fusion.6
  465.6 7.2 convolution_convert_fusion
  473.8 3.2 convolution_convert_fusion.8
  477.1 5.0 convolution_convert_fusion.5
  483.4 2.3 dynamic-slice_bitcast_fusion
  485.7 3.4 all-to-all-start.3
  489.8 14.7 %all-reduce.1 = f32[1024]{0:T(1024)S(1)} all-reduce(f32[1024]{0:T(1024)S(1)} %get-tuple-element.30), channel_id=10, replica_groups=mesh['seq'=4,'fsdp'=8] {'fsdp'}, use_global_device_ids=true, to_apply=%region_27.28.clone | all-reduce | flops 1024 | bytes 8192
  505.2 3.9 all-to-all-start.2
  510.6 29.0 %reduce-scatter.26.cloned.1.call-done = bf16[128,1024]{1,0:T(8,128)(2,1)} async-done(((bf16[1024,1024]{1,0:T(8,128)(2,1)}), bf16[128,1024]{1,0:T(8,128)(2,1)}) %reduce-scatter.26.cloned.1.call-update) | async-done | bytes 262160 | tf_op jit(solution)/shard_map/reduce_scatter | solution.py:134
  539.5 1.8 convert_element_type.209
  541.3 30.6 %reduce-scatter.24.cloned.1.call-done = bf16[32,1024]{1,0:T(8,128)(2,1)} async-done(((bf16[256,1024]{1,0:T(8,128)(2,1)}), bf16[32,1024]{1,0:T(8,128)(2,1)}) %reduce-scatter.24.cloned.1.call-update) | async-done | bytes 65552 | tf_op jit(solution)/shard_map/reduce_scatter | solution.py:134
  574.8 33.4 %reduce-scatter.20.cloned.1.call-done = bf16[256,1024]{1,0:T(8,128)(2,1)} async-done(((bf16[1024,1024]{1,0:T(8,128)(2,1)}), bf16[256,1024]{1,0:T(8,128)(2,1)}) %reduce-scatter.20.cloned.1.call-update) | async-done | bytes 524304 | tf_op jit(solution)/shard_map/reduce_scatter | solution.py:142
  612.4 132.6 %reduce-scatter.28.cloned.1.call-done = f32[32,8]{1,0:T(8,128)} async-done(((f32[1024,8]{1,0:T(8,128)}), f32[32,8]{1,0:T(8,128)}) %reduce-scatter.28.cloned.1.call-update) | async-done | bytes 1040
  (213 shorter events, 66.2 us)
Async XLA Ops:
  7.2 51.4 %copy-start = (bf16[1,256,1024]{2,1,0:T(8,128)(2,1)S(1)}, bf16[1,256,1024]{2,1,0:T(8,128)(2,1)}, u32[]{:S(2)}) copy-start(bf16[1,256,1024]{2,1,0:T(8,128)(2,1)} %param.16) | copy-start | bytes 1572868
  7.2 8.6 %copy-start.37 = (bf16[32]{0:T(256)(128)(2,1)S(1)}, bf16[32]{0:T(256)(128)(2,1)}, u32[]{:S(2)}) copy-start(bf16[32]{0:T(256)(128)(2,1)} %param.30) | copy-start | bytes 196
  7.2 8.6 %copy-start.36 = (bf16[32]{0:T(256)(128)(2,1)S(1)}, bf16[32]{0:T(256)(128)(2,1)}, u32[]{:S(2)}) copy-start(bf16[32]{0:T(256)(128)(2,1)} %param.29) | copy-start | bytes 196
  7.2 8.6 %copy-start.35 = (bf16[32]{0:T(256)(128)(2,1)S(1)}, bf16[32]{0:T(256)(128)(2,1)}, u32[]{:S(2)}) copy-start(bf16[32]{0:T(256)(128)(2,1)} %param.28) | copy-start | bytes 196
  7.2 8.6 %copy-start.34 = (bf16[32]{0:T(256)(128)(2,1)S(1)}, bf16[32]{0:T(256)(128)(2,1)}, u32[]{:S(2)}) copy-start(bf16[32]{0:T(256)(128)(2,1)} %param.27) | copy-start | bytes 196
  7.2 8.6 %copy-start.33 = (bf16[32]{0:T(256)(128)(2,1)S(1)}, bf16[32]{0:T(256)(128)(2,1)}, u32[]{:S(2)}) copy-start(bf16[32]{0:T(256)(128)(2,1)} %param.26) | copy-start | bytes 196
  7.2 8.6 %copy-start.32 = (bf16[32]{0:T(256)(128)(2,1)S(1)}, bf16[32]{0:T(256)(128)(2,1)}, u32[]{:S(2)}) copy-start(bf16[32]{0:T(256)(128)(2,1)} %param.25) | copy-start | bytes 196
  7.3 8.6 %copy-start.31 = (bf16[32]{0:T(256)(128)(2,1)S(1)}, bf16[32]{0:T(256)(128)(2,1)}, u32[]{:S(2)}) copy-start(bf16[32]{0:T(256)(128)(2,1)} %param.24) | copy-start | bytes 196
  7.3 8.6 %copy-start.30 = (bf16[32]{0:T(256)(128)(2,1)S(1)}, bf16[32]{0:T(256)(128)(2,1)}, u32[]{:S(2)}) copy-start(bf16[32]{0:T(256)(128)(2,1)} %param.23) | copy-start | bytes 196
  9.4 49.5 %all-to-all-start = ((bf16[4,32,768]{2,1,0:T(8,128)(2,1)}), bf16[4,32,768]{2,1,0:T(8,128)(2,1)S(1)}, u32[]{:S(2)}, u32[]{:S(2)}) async-start(bf16[4,32,768]{2,1,0:T(8,128)(2,1)} %reshape.367), calls=%async_computation | async-start | bytes 393216 | tf_op jit(solution)/shard_map/all_to_all | solution.py:121
  14.6 105.8 %all-gather.7.cloned.1.call-start = ((), (), s32[]{:S(2)}) async-start(), calls=%async_computation.12 | async-start | bytes 1769472 | tf_op jit(solution)/shard_map/all_gather | solution.py:122
  15.8 58.4 %copy-start.25 = (f32[256]{0:T(256)}, f32[256]{0:T(256)S(1)}, u32[]{:S(2)}) copy-start(f32[256]{0:T(256)S(1)} %broadcast_multiply_fusion.11) | copy-start | bytes 3076
  58.6 15.6 %copy-start.22 = (f32[1,1024]{1,0:T(1,128)}, f32[1,1024]{1,0:T(1,128)S(1)}, u32[]{:S(2)}) copy-start(f32[1,1024]{1,0:T(1,128)S(1)} %get-tuple-element.49) | copy-start | bytes 12292
  59.6 120.5 %reduce-scatter.14.cloned.1.call-start = ((), (), s32[]{:S(2)}) async-start(), calls=%async_computation.13 | async-start | bytes 2621440 | tf_op jit(solution)/shard_map/reduce_scatter | solution.py:142
  59.7 14.5 %copy-start.27 = (f32[256]{0:T(256)}, f32[256]{0:T(256)S(1)}, u32[]{:S(2)}) copy-start(f32[256]{0:T(256)S(1)} %add_rsqrt_fusion.3) | copy-start | bytes 3076
  60.0 14.2 %collective-permute-start = (bf16[1,256,1024]{2,1,0:T(8,128)(2,1)S(1)}, bf16[1,256,1024]{2,1,0:T(8,128)(2,1)S(1)}, u32[]{:S(2)}, u32[]{:S(2)}) collective-permute-start(bf16[1,256,1024]{2,1,0:T(8,128)(2,1)S(1)} %fusion.89), channel_id=1, source_target_pairs={{0,8},{8,0},{16,24},{24,16},{1,9},{9,1},{17,25},{25,17},{2,10},{10... | collective-permute-start | bytes 1572872 | tf_op jit(solution)/shard_map/ppermute | solution.py:24
  74.3 27.5 %copy-start.24 = (bf16[32,1024]{1,0:T(8,128)(2,1)S(1)}, bf16[32,1024]{1,0:T(8,128)(2,1)}, u32[]{:S(2)}) copy-start(bf16[32,1024]{1,0:T(8,128)(2,1)} %param.19) | copy-start | bytes 196612
  74.7 43.7 %collective-permute-start.1 = (bf16[2,256,1024]{2,1,0:T(8,128)(2,1)S(1)}, bf16[2,256,1024]{2,1,0:T(8,128)(2,1)}, u32[]{:S(2)}, u32[]{:S(2)}) collective-permute-start(bf16[2,256,1024]{2,1,0:T(8,128)(2,1)S(1)} %get-tuple-element.41), channel_id=1, source_target_pairs={{0,16},{8,24},{16,0},{24,8},{1,17},{9,25},{17,1},{25,9},{2,18},{10... | collective-permute-start | bytes 3145736 | tf_op jit(solution)/shard_map/ppermute | solution.py:24
  116.8 27.5 %copy-start.13 = (bf16[256,1024]{1,0:T(8,128)(2,1)}, bf16[256,1024]{1,0:T(8,128)(2,1)S(1)}, u32[]{:S(2)}) copy-start(bf16[256,1024]{1,0:T(8,128)(2,1)S(1)} %all_gather.24) | copy-start | bytes 1572868
  120.4 5.3 copy-start.5
  147.2 65.5 %all-gather.9.cloned.1.call-start = ((), (), s32[]{:S(2)}) async-start(), calls=%async_computation.14 | async-start | bytes 2359296 | tf_op jit(solution)/shard_map/all_gather | solution.py:122
  159.9 81.7 %all-gather.11.cloned.1.call-start = ((), (), s32[]{:S(2)}) async-start(), calls=%async_computation.15 | async-start | bytes 2359296 | tf_op jit(solution)/shard_map/all_gather | solution.py:165
  160.5 123.1 %reduce-scatter.16.cloned.1.call-start = ((), (), s32[]{:S(2)}) async-start(), calls=%async_computation.16 | async-start | bytes 2621440 | tf_op jit(solution)/shard_map/reduce_scatter | solution.py:142
  185.2 13.7 %collective-permute-start.2 = (bf16[1,256,1024]{2,1,0:T(8,128)(2,1)S(1)}, bf16[1,256,1024]{2,1,0:T(8,128)(2,1)S(1)}, u32[]{:S(2)}, u32[]{:S(2)}) collective-permute-start(bf16[1,256,1024]{2,1,0:T(8,128)(2,1)S(1)} %fusion.147), channel_id=1, source_target_pairs={{0,8},{8,0},{16,24},{24,16},{1,9},{9,1},{17,25},{25,17},{2,10},{10... | collective-permute-start | bytes 1572872 | tf_op jit(solution)/shard_map/ppermute | solution.py:24
  199.5 24.3 %collective-permute-start.3 = (bf16[2,256,1024]{2,1,0:T(8,128)(2,1)S(1)}, bf16[2,256,1024]{2,1,0:T(8,128)(2,1)}, u32[]{:S(2)}, u32[]{:S(2)}) collective-permute-start(bf16[2,256,1024]{2,1,0:T(8,128)(2,1)S(1)} %get-tuple-element.39), channel_id=1, source_target_pairs={{0,16},{8,24},{16,0},{24,8},{1,17},{9,25},{17,1},{25,9},{2,18},{10... | collective-permute-start | bytes 3145736 | tf_op jit(solution)/shard_map/ppermute | solution.py:24
  214.9 10.9 %copy-start.10 = (bf16[4,256,1024]{2,1,0:T(8,128)(2,1)}, bf16[4,256,1024]{2,1,0:T(8,128)(2,1)S(1)}, u32[]{:S(2)}) copy-start(bf16[4,256,1024]{2,1,0:T(8,128)(2,1)S(1)} %copy.89) | copy-start | bytes 6291460
  248.7 37.5 %copy-start.3 = (bf16[1,256,1024]{2,1,0:T(8,128)(2,1)S(1)}, bf16[1,256,1024]{2,1,0:T(8,128)(2,1)}, u32[]{:S(2)}) copy-start(bf16[1,256,1024]{2,1,0:T(8,128)(2,1)} %param.31) | copy-start | bytes 1572868
  248.7 126.8 %reduce-scatter.18.cloned.1.call-start = ((), (), s32[]{:S(2)}) async-start(), calls=%async_computation.17 | async-start | bytes 2621440 | tf_op jit(solution)/shard_map/reduce_scatter | solution.py:142
  283.6 4.2 copy-start.2
  288.2 13.7 %collective-permute-start.4 = (bf16[1,256,1024]{2,1,0:T(8,128)(2,1)S(1)}, bf16[1,256,1024]{2,1,0:T(8,128)(2,1)S(1)}, u32[]{:S(2)}, u32[]{:S(2)}) collective-permute-start(bf16[1,256,1024]{2,1,0:T(8,128)(2,1)S(1)} %fusion.145), channel_id=1, source_target_pairs={{0,8},{8,0},{16,24},{24,16},{1,9},{9,1},{17,25},{25,17},{2,10},{10... | collective-permute-start | bytes 1572872 | tf_op jit(solution)/shard_map/ppermute | solution.py:24
  302.3 24.1 %collective-permute-start.5 = (bf16[2,256,1024]{2,1,0:T(8,128)(2,1)S(1)}, bf16[2,256,1024]{2,1,0:T(8,128)(2,1)S(1)}, u32[]{:S(2)}, u32[]{:S(2)}) collective-permute-start(bf16[2,256,1024]{2,1,0:T(8,128)(2,1)S(1)} %get-tuple-element.37), channel_id=1, source_target_pairs={{0,16},{8,24},{16,0},{24,8},{1,17},{9,25},{17,1},{25,9},{2,18},{10... | collective-permute-start | bytes 3145736 | tf_op jit(solution)/shard_map/ppermute | solution.py:24
  327.2 8.0 %copy-start.9 = (bf16[2,2,256,1024]{3,2,1,0:T(8,128)(2,1)}, bf16[2,2,256,1024]{3,2,1,0:T(8,128)(2,1)S(1)}, u32[]{:S(2)}) copy-start(bf16[2,2,256,1024]{3,2,1,0:T(8,128)(2,1)S(1)} %reverse_select_fusion.1) | copy-start | bytes 6291460
  330.1 6.4 copy-start.11
  340.2 143.1 %all-reduce.4.cloned.1.call-start = ((), (), s32[]{:S(2)}) async-start(), calls=%async_computation.23 | async-start | bytes 4194304
  381.2 13.7 %collective-permute-start.6 = (bf16[1,256,1024]{2,1,0:T(8,128)(2,1)S(1)}, bf16[1,256,1024]{2,1,0:T(8,128)(2,1)S(1)}, u32[]{:S(2)}, u32[]{:S(2)}) collective-permute-start(bf16[1,256,1024]{2,1,0:T(8,128)(2,1)S(1)} %fusion.143), channel_id=1, source_target_pairs={{0,8},{8,0},{16,24},{24,16},{1,9},{9,1},{17,25},{25,17},{2,10},{10... | collective-permute-start | bytes 1572872 | tf_op jit(solution)/shard_map/ppermute | solution.py:24
  396.8 24.3 %collective-permute-start.7 = (bf16[2,256,1024]{2,1,0:T(8,128)(2,1)}, bf16[2,256,1024]{2,1,0:T(8,128)(2,1)}, u32[]{:S(2)}, u32[]{:S(2)}) collective-permute-start(bf16[2,256,1024]{2,1,0:T(8,128)(2,1)} %get-tuple-element.35), channel_id=1, source_target_pairs={{0,16},{8,24},{16,0},{24,8},{1,17},{9,25},{17,1},{25,9},{2,18},{10... | collective-permute-start | bytes 3145736 | tf_op jit(solution)/shard_map/ppermute | solution.py:24
  401.9 19.2 %copy-start.4 = (bf16[1,2,256,1024]{3,2,1,0:T(8,128)(2,1)S(1)}, bf16[1,2,256,1024]{3,2,1,0:T(8,128)(2,1)}, u32[]{:S(2)}) copy-start(bf16[1,2,256,1024]{3,2,1,0:T(8,128)(2,1)} %get-tuple-element.34) | copy-start | bytes 3145732
  401.9 103.3 %reduce-scatter.22.cloned.1.call-start = ((), (), s32[]{:S(2)}) async-start(), calls=%async_computation.19 | async-start | bytes 1769472 | tf_op jit(solution)/shard_map/reduce_scatter | solution.py:128
  424.5 8.7 %copy-start.18 = (bf16[1024,768]{0,1:T(8,128)(2,1)S(1)}, bf16[1024,768]{0,1:T(8,128)(2,1)}, u32[]{:S(2)}) copy-start(bf16[1024,768]{0,1:T(8,128)(2,1)} %convolution_convert_fusion.7) | copy-start | bytes 4718596
  465.3 74.2 %reduce-scatter.26.cloned.1.call-start = ((), (), s32[]{:S(2)}) async-start(), calls=%async_computation.21 | async-start | bytes 2359296 | tf_op jit(solution)/shard_map/reduce_scatter | solution.py:134
  472.8 99.1 %reduce-scatter.24.cloned.1.call-start = ((), (), s32[]{:S(2)}) async-start(), calls=%async_computation.20 | async-start | bytes 589824 | tf_op jit(solution)/shard_map/reduce_scatter | solution.py:134
  477.0 131.2 %reduce-scatter.20.cloned.1.call-start = ((), (), s32[]{:S(2)}) async-start(), calls=%async_computation.18 | async-start | bytes 2621440 | tf_op jit(solution)/shard_map/reduce_scatter | solution.py:142
  485.7 19.5 %all-to-all-start.3 = ((bf16[4,32,1024]{2,1,0:T(8,128)(2,1)}), bf16[4,32,1024]{2,1,0:T(8,128)(2,1)S(1)}, u32[]{:S(2)}, u32[]{:S(2)}) async-start(bf16[4,32,1024]{2,1,0:T(8,128)(2,1)} %dynamic-slice_bitcast_fusion), calls=%async_computation.9 | async-start | bytes 524288 | tf_op jit(solution)/shard_map/all_to_all | solution.py:129
  505.2 68.2 %all-to-all-start.2 = ((bf16[4,32,768]{2,1,0:T(8,128)(2,1)}), bf16[4,32,768]{2,1,0:T(8,128)(2,1)S(1)}, u32[]{:S(2)}, u32[]{:S(2)}) async-start(bf16[4,32,768]{2,1,0:T(8,128)(2,1)} %bitcast.344), calls=%async_computation.7 | async-start | bytes 393216 | tf_op jit(solution)/shard_map/all_to_all | solution.py:129
  509.0 236.0 %reduce-scatter.28.cloned.1.call-start = ((), (), s32[]{:S(2)}) async-start(), calls=%async_computation.22 | async-start | bytes 540672
  509.4 98.8 %copy-start.23 = (f32[1,1024]{1,0:T(1,128)S(1)}, f32[1,1024]{1,0:T(1,128)}, u32[]{:S(2)}) copy-start(f32[1,1024]{1,0:T(1,128)} %copy-done.22) | copy-start | bytes 12292
  509.4 98.8 %copy-start.26 = (f32[256]{0:T(256)S(1)}, f32[256]{0:T(256)}, u32[]{:S(2)}) copy-start(f32[256]{0:T(256)} %copy-done.25) | copy-start | bytes 3076
  509.4 98.8 %copy-start.28 = (f32[256]{0:T(256)S(1)}, f32[256]{0:T(256)}, u32[]{:S(2)}) copy-start(f32[256]{0:T(256)} %copy-done.27) | copy-start | bytes 3076
  (19 other events, 39.1 us)
Sparse Core Ops, SparseCore 0:
  59.7 21.4 all-gather.6
  147.4 32.6 reduce-scatter.13
  182.4 29.1 all-gather.8
  213.0 28.5 all-gather.10
  248.9 34.7 reduce-scatter.15
  340.4 35.1 reduce-scatter.17
  402.0 64.8 all-reduce.3
  469.3 33.6 reduce-scatter.21
  505.4 34.0 reduce-scatter.25
  542.3 29.5 reduce-scatter.23
  574.9 33.3 reduce-scatter.19
  611.2 133.8 reduce-scatter.27
